TPU v7x, 32 devices: a whole 2x2x4 slice. The times are simulated.
32 devices in a mesh: parts: 2 (over y), row: 4 (over z), col: 4 (over x, core).
Axes of the slice: x: 2, y: 2, z: 4, core: 2. Of those that a mesh axis runs over, the one named last changes fastest.
Arguments:
- amplitudes: bfloat16 [8, 100, 512, 512], P('parts', 'col', 'row'), parts along dimension 0, may hold values from -12 to 12
- integrals: bfloat16 [200, 512, 512], P(('parts', 'col'), 'row'), parts along dimension 0, may hold values from -0.109375 to 0.109375
- occ_irrep: int32 [200], P('parts'), parts along dimension 0, may hold values from 0 to 7, as said below
- vir_irrep: int32 [1024], P('parts'), parts along dimension 0, may hold values from 0 to 7, as said below
- screen: int32 [200, 8], P('parts'), parts along dimension 0, may hold values 0 or 1
- occ_energy: float32 [200], P('parts'), parts along dimension 0, may hold values from -1 to -0.3
- vir_energy: float32 [1024], P('parts'), parts along dimension 0, may hold values from 0.1 to 1
Outputs:
- update: float32 [512, 8, 512], P('row', 'parts', 'col'), parts along dimension 1
There are 2 independent parts, one for each index of `parts`. A program takes and returns all parts, laid end to end along the dimension named above; each array names one. Nothing has to cross between parts.
Inputs may be any that keep to these rules, and one draw needn't show every extreme that they name: `occ_irrep`: the labels never fall from one orbital to the next; the first is 0 and the last is 7. `vir_irrep`: the labels never fall from one orbital to the next and every label from 0 to 7 occurs; exactly one label covers 256 virtual orbitals, every other label fewer.
All inputs are finite; a program needn't handle non-finite values.
Results may differ from a plain program's by a relative error of at most 0.0003.
Values may be sent and summed in bfloat16 or wider, within the bound.
A program may use at most 128 MiB of HBM per device.

v0:
```python
import jax
import jax.numpy as jnp
from jax import lax
from jax.sharding import PartitionSpec as P


def folded_integrals(integrals, occ_local, vir_local, vir_irrep, screen_rows, pair_label):
    half = vir_irrep.shape[0] // 2
    irrep_codes = jnp.arange(8, dtype=jnp.int32)
    screen_local = jnp.sum(
        screen_rows[:, None, :] * (vir_local[None, :, None] == irrep_codes).astype(jnp.int32),
        axis=2,
    )
    wanted = jnp.bitwise_xor(jnp.bitwise_xor(occ_local[:, None], vir_local[None, :]), pair_label)
    wanted = jnp.where(screen_local == 1, wanted, -1)[:, :, None]
    zeros = jnp.zeros((), integrals.dtype)
    low = jnp.where(wanted == vir_irrep[None, None, :half], integrals[:, :, :half], zeros)
    return jnp.where(wanted == vir_irrep[None, None, half:], integrals[:, :, half:], low)


def on_device(amplitudes, integrals, occ_irrep, vir_irrep, screen, occ_energy, vir_energy):
    row_count = lax.axis_size("row")
    column_count = lax.axis_size("col")
    row, col = (lax.axis_index("row"), lax.axis_index("col"))
    batch_size, occ_share, vir_share, vir_total = amplitudes.shape
    half = vir_total // 2
    vir_columns = vir_total // column_count
    occ_offset = col * occ_share
    occ_local = lax.dynamic_slice_in_dim(occ_irrep, occ_offset, occ_share)
    vir_local = lax.dynamic_slice_in_dim(vir_irrep, row * vir_share, vir_share)
    screen_rows = lax.dynamic_slice_in_dim(screen, occ_offset, occ_share, 0)
    pair_label = occ_irrep[batch_size]
    folded = folded_integrals(integrals, occ_local, vir_local, vir_irrep, screen_rows, pair_label)
    gathered = lax.all_gather(folded, "row", axis=1, tiled=True)
    shift = jnp.bitwise_xor(occ_irrep[:batch_size, None], occ_local[None, :])
    keep_amp = (
        jnp.bitwise_xor(shift[:, :, None], vir_local[None, None, :])[:, :, :, None]
        == vir_irrep[None, None, None, :]
    )
    amp_kept = jnp.where(keep_amp, amplitudes, jnp.zeros_like(amplitudes))
    partial = lax.dot_general(
        amp_kept, gathered, (((1, 3), (0, 1)), ((), ())), preferred_element_type=jnp.float32
    )
    if row_count == column_count and column_count == 4:
        piece = lax.psum_scatter(partial, "col", scatter_dimension=2, tiled=True)
        routes = []
        for flip in (0, 1):
            pairs = []
            for r in range(row_count):
                for q in range(column_count):
                    target = q // 2 + 2 * ((q + flip) % 2)
                    pairs.append((r * column_count + q, target * column_count + r))
            routes.append(lax.ppermute(piece, ("row", "col"), pairs))
        swap = row // 2 == 1
        first = jnp.where(swap, routes[1], routes[0])
        second = jnp.where(swap, routes[0], routes[1])
        cycle = jnp.concatenate([first, second], axis=2)
    else:
        whole = lax.all_gather(lax.psum(partial, "col"), "row", axis=1, tiled=True)
        cycle = lax.dynamic_slice_in_dim(whole, col * vir_columns, vir_columns, 1)
        cycle = lax.dynamic_slice_in_dim(cycle, row * vir_share % half, vir_share, 2)
    cycle = jnp.transpose(cycle, (2, 0, 1))
    col_irrep = lax.dynamic_slice_in_dim(vir_irrep, col * vir_columns, vir_columns)
    kept = (
        jnp.bitwise_xor(occ_irrep[:batch_size, None], pair_label ^ col_irrep[None, :])[None]
        == vir_local[:, None, None]
    )
    cycle = jnp.where(kept, cycle, 0.0)
    energy_cols = lax.dynamic_slice_in_dim(vir_energy, col * vir_columns, vir_columns)
    energy_rows = lax.dynamic_slice_in_dim(vir_energy, row * vir_share, vir_share)
    denominator = (
        occ_energy[:batch_size][None, :, None]
        + occ_energy[batch_size]
        - energy_cols[None, None, :]
        - energy_rows[:, None, None]
    )
    return cycle / denominator


def solution(mesh):
    in_specs = (
        P("parts", "col", "row", None),
        P(("parts", "col"), "row", None),
        P("parts"),
        P("parts"),
        P("parts", None),
        P("parts"),
        P("parts"),
    )
    out_specs = P("row", "parts", "col")
    return jax.shard_map(
        on_device, mesh=mesh, in_specs=in_specs, out_specs=out_specs, check_vma=False
    )
```

profile of v0, /device:TPU:2, one launch (start us, length us, event | category | flops | bytes accessed | tf_op | source)
XLA Modules:
  0.0 192.5 jit_solution(17666716235107848208)
XLA Ops:
  6.5 1.2 slice.26
  7.8 0.8 fusion.14
  8.5 1.5 dynamic-slice_xor_fusion
  10.0 0.7 dynamic_slice.20
  10.8 0.1 copy.12
  10.9 3.4 %fusion.12 = (bf16[25,128,256]{2,1,0:T(8,128)(2,1)}, bf16[25,128,256]{2,1,0:T(8,128)(2,1)S(1)}) fusion(bf16[25,128,512]{2,1,0:T(8,128)(2,1)} %param.8), kind=kLoop, calls=%fused_computation.26 | loop fusion | bytes 6553600 | tf_op jit(solution)/shard_map/slice | solution.py:17
  14.4 2.1 %copy.17 = bf16[25,128,256]{1,2,0:T(8,128)(2,1)S(1)} copy(bf16[25,128,256]{2,1,0:T(8,128)(2,1)S(1)} %get-tuple-element.6) | data formatting | bytes 3276800
  16.5 3.1 %copy.18 = bf16[25,128,256]{1,2,0:T(8,128)(2,1)S(1)} copy(bf16[25,128,256]{2,1,0:T(8,128)(2,1)} %get-tuple-element.5) | data formatting | bytes 3276800
  19.6 0.1 multiply_reduce_fusion
  19.7 0.7 xor_select_fusion
  20.4 2.1 %compare_select_fusion.3 = bf16[25,128,256]{1,2,0:T(8,128)(2,1)} fusion(bf16[25,128,256]{1,2,0:T(8,128)(2,1)S(1)} %copy.17, bf16[25,128,256]{1,2,0:T(8,128)(2,1)S(1)} %copy.18, s32[25,128]{1,0:T(8,128)S(1)} %xor_select_fusion, s32[256]{0:T(256)S(1)} %get-tuple-element.14, s32[256]{0:T(256)S(1)} %get-tuple-element.13), kind=kLoop, calls=%fused_computation.7 | loop fusion | flops 3276800 | bytes 4930048 | tf_op jit(solution)/shard_map/jit(_where)/select_n | solution.py:18
  22.6 0.1 broadcast_xor_fusion
  22.7 10.7 %compare_select_fusion.8 = bf16[4,25,128,512]{3,2,1,0:T(8,128)(2,1)} fusion(bf16[4,25,128,512]{3,2,1,0:T(8,128)(2,1)} %param.7, s32[512]{0:T(512)S(1)} %copy-done.1, s32[4,25,128]{2,1,0:T(8,128)S(1)} %broadcast_xor_fusion), kind=kLoop, calls=%fused_computation.clone.clone.clone.clone.1 | loop fusion | flops 13107200 | bytes 26267648 | tf_op jit(solution)/shard_map/dot_general | solution.py:41
  33.4 109.6 %all-gather.2.cloned.1.call-done = bf16[25,512,256]{1,2,0:T(8,128)(2,1)} async-done(((bf16[25,128,256]{1,2,0:T(8,128)(2,1)}), bf16[25,512,256]{1,2,0:T(8,128)(2,1)}) %all-gather.2.cloned.1.call-update) | async-done | bytes 6553616 | tf_op jit(solution)/shard_map/all_gather | solution.py:34
  143.0 9.2 %fusion.5 = f32[4,128,256]{1,2,0:T(8,128)} fusion(bf16[25,512,256]{1,2,0:T(8,128)(2,1)} %all-gather.2.cloned.1.call-done, bf16[4,25,128,512]{3,2,1,0:T(8,128)(2,1)} %compare_select_fusion.8), kind=kOutput, calls=%fused_computation.8 | convolution fusion | flops 3355443200 | bytes 20185088 | tf_op jit(solution)/shard_map/dot_general | solution.py:41
  152.3 0.6 slice.32
  153.0 0.6 slice_add_fusion
  153.7 17.4 %reduce-scatter.2.cloned.1.call-done = f32[4,128,64]{1,2,0:T(8,128)} async-done(((f32[4,128,256]{1,2,0:T(8,128)}), f32[4,128,64]{1,2,0:T(8,128)}) %reduce-scatter.2.cloned.1.call-update) | async-done | bytes 131088 | tf_op jit(solution)/shard_map/reduce_scatter | solution.py:45
  171.1 4.5 %collective-permute-start = (f32[4,128,64]{1,2,0:T(8,128)}, f32[4,128,64]{1,2,0:T(8,128)S(1)}, u32[]{:S(2)}, u32[]{:S(2)}) collective-permute-start(f32[4,128,64]{1,2,0:T(8,128)} %reduce-scatter.2.cloned.1.call-done), channel_id=1, source_target_pairs={{0,8},{1,0},{2,12},{3,4},{4,9},{5,1},{6,13},{7,5},{8,10},{9,2},{10... | collective-permute-start | bytes 393224 | tf_op jit(solution)/shard_map/ppermute | solution.py:53
  175.6 1.9 collective-permute-start.1
  177.6 1.5 collective-permute-done
  179.0 5.6 %collective-permute-done.1 = f32[4,128,64]{1,2,0:T(8,128)S(1)} collective-permute-done((f32[4,128,64]{1,2,0:T(8,128)}, f32[4,128,64]{1,2,0:T(8,128)S(1)}, u32[]{:S(2)}, u32[]{:S(2)}) %collective-permute-start.1) | collective-permute-done | bytes 131104 | tf_op jit(solution)/shard_map/ppermute | solution.py:53
  184.7 0.1 fusion.9
  184.8 0.9 copy.15
  (21 shorter events, 0.5 us)
Async XLA Ops:
  6.5 4.2 %copy-start = (s32[100,8]{0,1:T(8,128)S(1)}, s32[100,8]{0,1:T(8,128)}, u32[]{:S(2)}) copy-start(s32[100,8]{0,1:T(8,128)} %param.11) | copy-start | bytes 9604
  6.5 136.5 %all-gather.2.cloned.1.call-start = ((), (), s32[]{:S(2)}) async-start(), calls=%async_computation.1 | async-start | bytes 8192000 | tf_op jit(solution)/shard_map/all_gather | solution.py:34
  20.4 2.1 %copy-start.2 = (s32[100]{0:T(128)S(1)}, s32[100]{0:T(128)}, u32[]{:S(2)}) copy-start(s32[100]{0:T(128)} %param.9) | copy-start | bytes 1204
  20.4 2.3 %copy-start.1 = (s32[512]{0:T(512)S(1)}, s32[512]{0:T(512)}, u32[]{:S(2)}) copy-start(s32[512]{0:T(512)} %param.10) | copy-start | bytes 6148
  22.5 148.6 %reduce-scatter.2.cloned.1.call-start = ((), (), s32[]{:S(2)}) async-start(), calls=%async_computation.2 | async-start | bytes 655360 | tf_op jit(solution)/shard_map/reduce_scatter | solution.py:45
  33.4 118.8 %copy-start.4 = (f32[100]{0:T(128)S(1)}, f32[100]{0:T(128)}, u32[]{:S(2)}) copy-start(f32[100]{0:T(128)} %param.12) | copy-start | bytes 1204
  33.4 119.4 %copy-start.3 = (f32[512]{0:T(512)S(1)}, f32[512]{0:T(512)}, u32[]{:S(2)}) copy-start(f32[512]{0:T(512)} %param.13) | copy-start | bytes 6148
  171.1 7.9 %collective-permute-start = (f32[4,128,64]{1,2,0:T(8,128)}, f32[4,128,64]{1,2,0:T(8,128)S(1)}, u32[]{:S(2)}, u32[]{:S(2)}) collective-permute-start(f32[4,128,64]{1,2,0:T(8,128)} %reduce-scatter.2.cloned.1.call-done), channel_id=1, source_target_pairs={{0,8},{1,0},{2,12},{3,4},{4,9},{5,1},{6,13},{7,5},{8,10},{9,2},{10... | collective-permute-start | bytes 393224 | tf_op jit(solution)/shard_map/ppermute | solution.py:53
  175.6 9.0 %collective-permute-start.1 = (f32[4,128,64]{1,2,0:T(8,128)}, f32[4,128,64]{1,2,0:T(8,128)S(1)}, u32[]{:S(2)}, u32[]{:S(2)}) collective-permute-start(f32[4,128,64]{1,2,0:T(8,128)} %reduce-scatter.2.cloned.1.call-done), channel_id=1, source_target_pairs={{0,0},{1,8},{2,4},{3,12},{4,1},{5,9},{6,5},{7,13},{8,2},{9,10},{10... | collective-permute-start | bytes 393224 | tf_op jit(solution)/shard_map/ppermute | solution.py:53
Sparse Core Ops, SparseCore 0:
  22.6 120.3 all-gather.1
  152.4 18.6 reduce-scatter.1
where the time goes:
time: 193 us; the launch traced here: 192 us
  waiting for transfers between devices  134 us (69%)
  other arithmetic  16.1 us (8%)
  between operations  13.5 us (7%)
  local copies, waits for them, and re-layouts  13.1 us (7%)
  matrix products  9.22 us (5%)
  starting transfers between devices  6.42 us (3%)
    all_gather x1, waiting for transfers between devices, on_device(): gathered = lax.all_gather(folded, 'row', axis=1, tiled=True)  110 us
    reduce_scatter x1, waiting for transfers between devices, on_device(): piece = lax.psum_scatter(partial, 'col', scatter_dimension=2, tiled=True)  17.4 us
    dot_general x1, other arithmetic, on_device(): lax.dot_general(amp_kept, gathered, (((1, 3), (0, 1)), ((), ())), preferr...  10.7 us
    dot_general x1, matrix products, on_device(): lax.dot_general(amp_kept, gathered, (((1, 3), (0, 1)), ((), ())), preferr...  9.22 us
    ppermute x2, waiting for transfers between devices, on_device(): routes.append(lax.ppermute(piece, ('row', 'col'), pairs))  7.05 us
    ppermute x2, starting transfers between devices, on_device(): routes.append(lax.ppermute(piece, ('row', 'col'), pairs))  6.37 us
    unnamed x12, local copies, waits for them, and re-layouts  5.25 us
  transfers between devices with their start and end apart: 4, of which 4 were waited for; matrix products, arithmetic and copies ran while one was open for 6% of the time, Pallas kernels for 0%

commit v1 on v0

--- a/solution.py
+++ b/solution.py
@@ -1,7 +1,32 @@
+import functools
 import jax
 import jax.numpy as jnp
 from jax import lax
 from jax.sharding import PartitionSpec as P
+
+
+def _raise_yards(x_in, out_dim):
+    tmp = lax.axis_index("row")
+    g_now = lax.axis_size("row")
+    u1, earlier, reached = (g_now, tmp, x_in.shape[out_dim])
+    rows = [to_i * u1 if j0 == out_dim else to_i for j0, to_i in enumerate(x_in.shape)]
+    y = jnp.zeros(rows, x_in.dtype)
+    piece_out = z_new = x_in
+    after = lax.dynamic_update_slice_in_dim(y, x_in, earlier * reached, axis=out_dim)
+    for w in range(1, u1 // 2 + 1):
+        piece_out = lax.ppermute(piece_out, "row", [(j0, (j0 + 1) % u1) for j0 in range(u1)])
+        after = lax.dynamic_update_slice_in_dim(
+            after, piece_out, (earlier - w) % u1 * reached, axis=out_dim
+        )
+        if 2 * w < u1:
+            z_new = lax.ppermute(z_new, "row", [(j0, (j0 - 1) % u1) for j0 in range(u1)])
+            after = lax.dynamic_update_slice_in_dim(
+                after, z_new, (earlier + w) % u1 * reached, axis=out_dim
+            )
+    return after
+
+
+_search_record = functools.partial(_raise_yards, out_dim=1)
 
 
 def folded_integrals(integrals, occ_local, vir_local, vir_irrep, screen_rows, pair_label):
@@ -31,7 +56,7 @@
     screen_rows = lax.dynamic_slice_in_dim(screen, occ_offset, occ_share, 0)
     pair_label = occ_irrep[batch_size]
     folded = folded_integrals(integrals, occ_local, vir_local, vir_irrep, screen_rows, pair_label)
-    gathered = lax.all_gather(folded, "row", axis=1, tiled=True)
+    gathered = _search_record(folded)
     shift = jnp.bitwise_xor(occ_irrep[:batch_size, None], occ_local[None, :])
     keep_amp = (
         jnp.bitwise_xor(shift[:, :, None], vir_local[None, None, :])[:, :, :, None]

time: 193 us -> 180 us (0.933)
  waiting for transfers between devices: 134 us -> 105 us
  local copies, waits for them, and re-layouts: 13.1 us -> 24.8 us
  starting transfers between devices: 6.42 us -> 10.3 us
    all_gather x1 -> x0, waiting for transfers between devices: 110 us -> none  [on_device(): gathered = lax.all_gather(folded, 'row', axis=1, tiled=True)]
    ppermute x0 -> x3, waiting for transfers between devices: none -> 79.4 us  [the longest x2 59.1 us: _raise_yards(): lax.ppermute(piece_out, 'row', [(j0, (j0 + 1) % u1) for j0 in range(u1)])]
    ppermute x0 -> x3, local copies, waits for them, and re-layouts: none -> 9.35 us  [the longest x2 6.23 us: _raise_yards(): lax.ppermute(piece_out, 'row', [(j0, (j0 + 1) % u1) for j0 in range(u1)])]
    dynamic_update_slice x0 -> x4, local copies, waits for them, and re-layouts: none -> 5.42 us  [the longest x2 2.74 us: _raise_yards(): lax.dynamic_update_slice_in_dim(after, piece_out, (earlier - w) % u1 * re...]
    unnamed x12 -> x10, local copies, waits for them, and re-layouts: 5.25 us -> 0.02 us
    ppermute x0 -> x3, starting transfers between devices: none -> 3.88 us  [the longest x1 2.25 us: _raise_yards(): lax.ppermute(z_new, 'row', [(j0, (j0 - 1) % u1) for j0 in range(u1)])]
    slice x1 -> x0, local copies, waits for them, and re-layouts: 3.42 us -> none  [folded_integrals(): integrals[:, :, :half]]
    broadcast_in_dim x0 -> x1, local copies, waits for them, and re-layouts: none -> 3.41 us  [_raise_yards(): y = jnp.zeros(rows, x_in.dtype)]
  transfers between devices with their start and end apart: 4 -> 6, of which waited for: 4 -> 6; matrix products, arithmetic and copies ran while one was open for 6% -> 16% of each run, Pallas kernels for 0% -> 0%
where the time goes in v1:
time: 180 us; the launch traced here: 179 us
  waiting for transfers between devices  105 us (58%)
  local copies, waits for them, and re-layouts  24.8 us (14%)
  other arithmetic  16.4 us (9%)
  between operations  13.5 us (8%)
  starting transfers between devices  10.3 us (6%)
  matrix products  9.24 us (5%)
    ppermute x2, waiting for transfers between devices, _raise_yards(): lax.ppermute(piece_out, 'row', [(j0, (j0 + 1) % u1) for j0 in range(u1)])  59.1 us
    ppermute x1, waiting for transfers between devices, _raise_yards(): lax.ppermute(z_new, 'row', [(j0, (j0 - 1) % u1) for j0 in range(u1)])  20.2 us
    reduce_scatter x1, waiting for transfers between devices, on_device(): piece = lax.psum_scatter(partial, 'col', scatter_dimension=2, tiled=True)  18.6 us
    dot_general x1, other arithmetic, on_device(): lax.dot_general(amp_kept, gathered, (((1, 3), (0, 1)), ((), ())), preferr...  10.5 us
    dot_general x1, matrix products, on_device(): lax.dot_general(amp_kept, gathered, (((1, 3), (0, 1)), ((), ())), preferr...  9.24 us
    ppermute x2, waiting for transfers between devices, on_device(): routes.append(lax.ppermute(piece, ('row', 'col'), pairs))  7.03 us
    ppermute x2, starting transfers between devices, on_device(): routes.append(lax.ppermute(piece, ('row', 'col'), pairs))  6.39 us
    ppermute x2, local copies, waits for them, and re-layouts, _raise_yards(): lax.ppermute(piece_out, 'row', [(j0, (j0 + 1) % u1) for j0 in range(u1)])  6.23 us
  transfers between devices with their start and end apart: 6, of which 6 were waited for; matrix products, arithmetic and copies ran while one was open for 16% of the time, Pallas kernels for 0%

profile of v1, /device:TPU:2, one launch (start us, length us, event | category | flops | bytes accessed | tf_op | source)
XLA Modules:
  0.0 179.2 jit_solution(16281473984480083370)
XLA Ops:
  6.5 1.3 slice.26
  8.6 1.5 dynamic-slice_xor_fusion
  11.8 2.4 %compare_select_fusion.3 = bf16[25,128,256]{2,1,0:T(8,128)(2,1)S(1)} fusion(bf16[25,128,512]{2,1,0:T(8,128)(2,1)} %param.8, s32[256]{0:T(256)S(1)} %get-tuple-element.12, s32[256]{0:T(256)S(1)} %get-tuple-element.11, s32[25,128]{1,0:T(8,128)S(1)} %xor_select_fusion), kind=kLoop, calls=%fused_computation.7 | loop fusion | flops 3276800 | bytes 4930048 | tf_op jit(solution)/shard_map/jit(_where)/select_n | solution.py:43
  14.3 1.6 collective-permute-start
  15.9 2.2 %collective-permute-start.1 = (bf16[25,128,256]{2,1,0:T(8,128)(2,1)S(1)}, bf16[25,128,256]{2,1,0:T(8,128)(2,1)}, u32[]{:S(2)}, u32[]{:S(2)}) collective-permute-start(bf16[25,128,256]{2,1,0:T(8,128)(2,1)S(1)} %compare_select_fusion.3), channel_id=1, source_target_pairs={{0,12},{4,0},{8,4},{12,8},{1,13},{5,1},{9,5},{13,9},{2,14},{6,2},{... | collective-permute-start | bytes 4915208 | tf_op jit(solution)/shard_map/ppermute | solution.py:22
  18.1 2.1 %copy.15 = bf16[25,128,256]{1,2,0:T(8,128)(2,1)S(1)} copy(bf16[25,128,256]{2,1,0:T(8,128)(2,1)S(1)} %compare_select_fusion.3) | data formatting | bytes 3276800 | tf_op jit(solution)/shard_map/jit(_where)/select_n | solution.py:43
  20.4 3.4 %broadcast_in_dim.16 = bf16[25,512,256]{1,2,0:T(8,128)(2,1)} broadcast(bf16[]{:T(256)} %constant.57.clone.1), dimensions={} | broadcast | bytes 6553602 | tf_op jit(solution)/shard_map/broadcast_in_dim | solution.py:13
  23.8 1.4 constant_dynamic-update-slice_fusion.3
  25.2 29.7 %collective-permute-done = bf16[25,128,256]{2,1,0:T(8,128)(2,1)} collective-permute-done((bf16[25,128,256]{2,1,0:T(8,128)(2,1)S(1)}, bf16[25,128,256]{2,1,0:T(8,128)(2,1)}, u32[]{:S(2)}, u32[]{:S(2)}) %collective-permute-start) | collective-permute-done | bytes 1638432 | tf_op jit(solution)/shard_map/ppermute | solution.py:17
  55.0 10.5 %compare_select_fusion.8 = bf16[4,25,128,512]{3,2,1,0:T(8,128)(2,1)} fusion(bf16[4,25,128,512]{3,2,1,0:T(8,128)(2,1)} %param.7, s32[512]{0:T(512)S(1)} %copy-done.1, s32[4,25,128]{2,1,0:T(8,128)S(1)} %broadcast_xor_fusion), kind=kLoop, calls=%fused_computation.clone.clone.clone.clone.1 | loop fusion | flops 13107200 | bytes 26267648 | tf_op jit(solution)/shard_map/dot_general | solution.py:66
  65.5 3.1 %copy.16 = bf16[25,128,256]{1,2,0:T(8,128)(2,1)S(1)} copy(bf16[25,128,256]{2,1,0:T(8,128)(2,1)} %collective-permute-done) | data formatting | bytes 3276800 | tf_op jit(solution)/shard_map/ppermute | solution.py:17
  68.6 20.2 %collective-permute-done.1 = bf16[25,128,256]{2,1,0:T(8,128)(2,1)} collective-permute-done((bf16[25,128,256]{2,1,0:T(8,128)(2,1)S(1)}, bf16[25,128,256]{2,1,0:T(8,128)(2,1)}, u32[]{:S(2)}, u32[]{:S(2)}) %collective-permute-start.1) | collective-permute-done | bytes 1638432 | tf_op jit(solution)/shard_map/ppermute | solution.py:22
  88.8 3.1 %copy.17 = bf16[25,128,256]{1,2,0:T(8,128)(2,1)S(1)} copy(bf16[25,128,256]{2,1,0:T(8,128)(2,1)} %collective-permute-done.1) | data formatting | bytes 3276800 | tf_op jit(solution)/shard_map/ppermute | solution.py:22
  92.0 1.4 constant_dynamic-update-slice_fusion.2
  93.4 1.3 constant_dynamic-update-slice_fusion.1
  94.7 29.4 %collective-permute-done.2 = bf16[25,128,256]{2,1,0:T(8,128)(2,1)} collective-permute-done((bf16[25,128,256]{2,1,0:T(8,128)(2,1)}, bf16[25,128,256]{2,1,0:T(8,128)(2,1)}, u32[]{:S(2)}, u32[]{:S(2)}) %collective-permute-start.2) | collective-permute-done | bytes 1638432 | tf_op jit(solution)/shard_map/ppermute | solution.py:17
  124.1 3.1 %copy.18 = bf16[25,128,256]{1,2,0:T(8,128)(2,1)S(1)} copy(bf16[25,128,256]{2,1,0:T(8,128)(2,1)} %collective-permute-done.2) | data formatting | bytes 3276800 | tf_op jit(solution)/shard_map/ppermute | solution.py:17
  127.2 1.3 constant_dynamic-update-slice_fusion
  128.6 9.2 %fusion.5 = f32[4,128,256]{1,2,0:T(8,128)} fusion(bf16[25,512,256]{1,2,0:T(8,128)(2,1)} %constant_dynamic-update-slice_fusion, bf16[4,25,128,512]{3,2,1,0:T(8,128)(2,1)} %compare_select_fusion.8), kind=kOutput, calls=%fused_computation.8 | convolution fusion | flops 3355443200 | bytes 20185088 | tf_op jit(solution)/shard_map/dot_general | solution.py:66
  139.2 18.6 %reduce-scatter.2.cloned.1.call-done = f32[4,128,64]{1,2,0:T(8,128)} async-done(((f32[4,128,256]{1,2,0:T(8,128)}), f32[4,128,64]{1,2,0:T(8,128)}) %reduce-scatter.2.cloned.1.call-update) | async-done | bytes 131088 | tf_op jit(solution)/shard_map/reduce_scatter | solution.py:70
  157.8 4.5 %collective-permute-start.3 = (f32[4,128,64]{1,2,0:T(8,128)}, f32[4,128,64]{1,2,0:T(8,128)S(1)}, u32[]{:S(2)}, u32[]{:S(2)}) collective-permute-start(f32[4,128,64]{1,2,0:T(8,128)} %reduce-scatter.2.cloned.1.call-done), channel_id=1, source_target_pairs={{0,8},{1,0},{2,12},{3,4},{4,9},{5,1},{6,13},{7,5},{8,10},{9,2},{10... | collective-permute-start | bytes 393224 | tf_op jit(solution)/shard_map/ppermute | solution.py:78
  162.3 1.9 %collective-permute-start.4 = (f32[4,128,64]{1,2,0:T(8,128)}, f32[4,128,64]{1,2,0:T(8,128)S(1)}, u32[]{:S(2)}, u32[]{:S(2)}) collective-permute-start(f32[4,128,64]{1,2,0:T(8,128)} %reduce-scatter.2.cloned.1.call-done), channel_id=1, source_target_pairs={{0,0},{1,8},{2,4},{3,12},{4,1},{5,9},{6,5},{7,13},{8,2},{9,10},{10... | collective-permute-start | bytes 393224 | tf_op jit(solution)/shard_map/ppermute | solution.py:78
  164.3 1.4 collective-permute-done.3
  165.7 5.6 %collective-permute-done.4 = f32[4,128,64]{1,2,0:T(8,128)S(1)} collective-permute-done((f32[4,128,64]{1,2,0:T(8,128)}, f32[4,128,64]{1,2,0:T(8,128)S(1)}, u32[]{:S(2)}, u32[]{:S(2)}) %collective-permute-start.4) | collective-permute-done | bytes 131104 | tf_op jit(solution)/shard_map/ppermute | solution.py:78
  (30 shorter events, 5.1 us)
Async XLA Ops:
  6.5 4.3 %copy-start = (s32[100,8]{0,1:T(8,128)S(1)}, s32[100,8]{0,1:T(8,128)}, u32[]{:S(2)}) copy-start(s32[100,8]{0,1:T(8,128)} %param.11) | copy-start | bytes 9604
  6.5 13.7 %copy-start.2 = (s32[100]{0:T(128)S(1)}, s32[100]{0:T(128)}, u32[]{:S(2)}) copy-start(s32[100]{0:T(128)} %param.9) | copy-start | bytes 1204
  6.5 151.3 %reduce-scatter.2.cloned.1.call-start = ((), (), s32[]{:S(2)}) async-start(), calls=%async_computation.1 | async-start | bytes 655360 | tf_op jit(solution)/shard_map/reduce_scatter | solution.py:70
  14.3 40.7 %copy-start.1 = (s32[512]{0:T(512)S(1)}, s32[512]{0:T(512)}, u32[]{:S(2)}) copy-start(s32[512]{0:T(512)} %param.10) | copy-start | bytes 6148
  14.3 40.7 %collective-permute-start = (bf16[25,128,256]{2,1,0:T(8,128)(2,1)S(1)}, bf16[25,128,256]{2,1,0:T(8,128)(2,1)}, u32[]{:S(2)}, u32[]{:S(2)}) collective-permute-start(bf16[25,128,256]{2,1,0:T(8,128)(2,1)S(1)} %compare_select_fusion.3), channel_id=1, source_target_pairs={{0,4},{4,8},{8,12},{12,0},{1,5},{5,9},{9,13},{13,1},{2,6},{6,10},{... | collective-permute-start | bytes 4915208 | tf_op jit(solution)/shard_map/ppermute | solution.py:17
  15.9 72.9 %collective-permute-start.1 = (bf16[25,128,256]{2,1,0:T(8,128)(2,1)S(1)}, bf16[25,128,256]{2,1,0:T(8,128)(2,1)}, u32[]{:S(2)}, u32[]{:S(2)}) collective-permute-start(bf16[25,128,256]{2,1,0:T(8,128)(2,1)S(1)} %compare_select_fusion.3), channel_id=1, source_target_pairs={{0,12},{4,0},{8,4},{12,8},{1,13},{5,1},{9,5},{13,9},{2,14},{6,2},{... | collective-permute-start | bytes 4915208 | tf_op jit(solution)/shard_map/ppermute | solution.py:22
  55.0 69.1 %collective-permute-start.2 = (bf16[25,128,256]{2,1,0:T(8,128)(2,1)}, bf16[25,128,256]{2,1,0:T(8,128)(2,1)}, u32[]{:S(2)}, u32[]{:S(2)}) collective-permute-start(bf16[25,128,256]{2,1,0:T(8,128)(2,1)} %collective-permute-done), channel_id=1, source_target_pairs={{0,4},{4,8},{8,12},{12,0},{1,5},{5,9},{9,13},{13,1},{2,6},{6,10},{... | collective-permute-start | bytes 4915208 | tf_op jit(solution)/shard_map/ppermute | solution.py:17
  128.6 9.3 %copy-start.4 = (f32[100]{0:T(128)S(1)}, f32[100]{0:T(128)}, u32[]{:S(2)}) copy-start(f32[100]{0:T(128)} %param.12) | copy-start | bytes 1204
  128.6 9.9 %copy-start.3 = (f32[512]{0:T(512)S(1)}, f32[512]{0:T(512)}, u32[]{:S(2)}) copy-start(f32[512]{0:T(512)} %param.13) | copy-start | bytes 6148
  157.8 7.9 %collective-permute-start.3 = (f32[4,128,64]{1,2,0:T(8,128)}, f32[4,128,64]{1,2,0:T(8,128)S(1)}, u32[]{:S(2)}, u32[]{:S(2)}) collective-permute-start(f32[4,128,64]{1,2,0:T(8,128)} %reduce-scatter.2.cloned.1.call-done), channel_id=1, source_target_pairs={{0,8},{1,0},{2,12},{3,4},{4,9},{5,1},{6,13},{7,5},{8,10},{9,2},{10... | collective-permute-start | bytes 393224 | tf_op jit(solution)/shard_map/ppermute | solution.py:78
  162.3 9.0 %collective-permute-start.4 = (f32[4,128,64]{1,2,0:T(8,128)}, f32[4,128,64]{1,2,0:T(8,128)S(1)}, u32[]{:S(2)}, u32[]{:S(2)}) collective-permute-start(f32[4,128,64]{1,2,0:T(8,128)} %reduce-scatter.2.cloned.1.call-done), channel_id=1, source_target_pairs={{0,0},{1,8},{2,4},{3,12},{4,1},{5,9},{6,5},{7,13},{8,2},{9,10},{10... | collective-permute-start | bytes 393224 | tf_op jit(solution)/shard_map/ppermute | solution.py:78
Sparse Core Ops, SparseCore 0:
  137.9 19.8 reduce-scatter.1
